TPU v7x, 512 devices: a whole 4x8x8 slice. The times are simulated.
512 devices in a mesh: ctx: 32 (over z_hi, x, core), head: 16 (over y, z_lo).
Axes of the slice: x: 4, y: 8, z: 8 (z_hi: 4, z_lo: 2; z = z_hi * 2 + z_lo), core: 2. Of those that a mesh axis runs over, the one named last changes fastest.
Arguments:
- queries: bfloat16 [32768, 2048], P('ctx', 'head'), may hold values from -4.5 to 4.5
- keys: bfloat16 [32768, 2048], P('ctx', 'head'), may hold values from -4.5 to 4.5
- values: bfloat16 [32768, 2048], P('ctx', 'head'), may hold values from -6 to 6
- out_weight: bfloat16 [2048, 2048], P('head'), may hold values from -0.5 to 0.5
Outputs:
- mixed: bfloat16 [32768, 2048], P(('ctx', 'head'))
All inputs are finite; a program needn't handle non-finite values.
Results may differ from a plain program's by a relative error of at most 0.019.
Values may be sent and summed in bfloat16 or wider, within the bound.
A program may use at most 64 MiB of HBM per device.

v0:
```python
import jax
import jax.numpy as jnp
from jax import lax
from jax.sharding import PartitionSpec as P

HEAD_SIZE = 128
WINDOW = 512
STRIDE = 16
BLOCK = 128
SUMCOLS = 8


BIG_NEG = -1e30


def from_behind(value, axis, steps):
    count = lax.axis_size(axis)
    initial, last = (max(0, -steps), min(count, count - steps))
    return lax.ppermute(value, axis, [(source, source + steps) for source in range(initial, last)])


def softmax_weighted(logit_scores, permitted_mask, value_rows, form):
    masked = jnp.where(permitted_mask, logit_scores, BIG_NEG)
    row_top = jnp.max(masked, axis=-1, keepdims=True)
    exponent = jnp.where(permitted_mask, jnp.exp(masked - row_top), 0.0)
    total = jnp.sum(exponent, axis=-1, keepdims=True)
    result = jnp.einsum(
        form, exponent.astype(jnp.bfloat16), value_rows, preferred_element_type=jnp.float32
    )
    return result / total


def local_section(query, key_rows, value_rows, score_scale):
    tokens_dev, heads_dev, head_dim = query.shape
    blocks = tokens_dev // WINDOW
    rim_rows = jnp.stack([key_rows[tokens_dev - WINDOW :], value_rows[tokens_dev - WINDOW :]])
    before = from_behind(rim_rows, "ctx", 1)
    key_ext = jnp.concatenate([before[0], key_rows]).reshape(
        blocks + 1, WINDOW, heads_dev, head_dim
    )
    value_ext = jnp.concatenate([before[1], value_rows]).reshape(
        blocks + 1, WINDOW, heads_dev, head_dim
    )
    paired_keys = jnp.concatenate([key_ext[:-1], key_ext[1:]], axis=1)
    paired_values = jnp.concatenate([value_ext[:-1], value_ext[1:]], axis=1)
    query_block_rows = query.reshape(blocks, WINDOW, heads_dev, head_dim)
    logit_scores = (
        jnp.einsum(
            "bqhd,bkhd->bhqk", query_block_rows, paired_keys, preferred_element_type=jnp.float32
        )
        * score_scale
    )
    block_ids = jnp.arange(blocks)[:, None, None, None]
    row_ids = jnp.arange(WINDOW)[None, None, :, None]
    col_ids = jnp.arange(2 * WINDOW)[None, None, None, :]
    first = lax.axis_index("ctx") * tokens_dev
    query_pos = block_ids * WINDOW + row_ids
    key_pos = (block_ids - 1) * WINDOW + col_ids
    permitted_mask = (
        (key_pos <= query_pos) & (key_pos > query_pos - WINDOW) & (key_pos + first >= 0)
    )
    result = softmax_weighted(logit_scores, permitted_mask, paired_values, "bhqk,bkhd->bhqd")
    return jnp.transpose(result, (0, 2, 1, 3)).reshape(tokens_dev, heads_dev, head_dim)


def phase_attend(phase_query, phase_keys, phase_values, query_pos, key_pos, score_scale):
    rows_total, per_device, heads_dev, head_dim = phase_query.shape
    step_rows = min(rows_total, 512)
    count_blocks = rows_total // step_rows
    query_block_rows = phase_query.reshape(count_blocks, step_rows, per_device, heads_dev, head_dim)
    position_blocks = query_pos.reshape(count_blocks, step_rows)

    def phase_one_block(operands):
        block_query, block_pos = operands
        logit_scores = (
            jnp.einsum(
                "qehd,kehd->ehqk", block_query, phase_keys, preferred_element_type=jnp.float32
            )
            * score_scale
        )
        permitted_mask = (key_pos[None, :] <= block_pos[:, None])[None, None]
        result = softmax_weighted(logit_scores, permitted_mask, phase_values, "ehqk,kehd->ehqd")
        return jnp.transpose(result, (2, 0, 1, 3))

    result = lax.map(phase_one_block, (query_block_rows, position_blocks))
    return result.reshape(rows_total, per_device, heads_dev, head_dim)


def stride_section(query, key_rows, value_rows, score_scale):
    tokens_dev, heads_dev, head_dim = query.shape
    width = heads_dev * head_dim
    ctx_count = lax.axis_size("ctx")
    copies = max(ctx_count // STRIDE, 1)
    per_device = max(STRIDE // ctx_count, 1)
    groups = STRIDE // per_device
    row_count = tokens_dev // STRIDE
    held_rows = ctx_count * row_count // copies
    own_copy = lax.axis_index("ctx") // groups
    source = jnp.arange(held_rows) // (row_count // copies)
    within = jnp.arange(held_rows) % (row_count // copies)
    query_pos = source * row_count + within * copies + own_copy
    shaped = query.reshape(1, row_count // copies, copies, groups, per_device, width)
    shaped = shaped.reshape(1, row_count // copies, ctx_count, per_device, width)
    moved = lax.all_to_all(shaped, "ctx", split_axis=2, concat_axis=1, tiled=True)
    phase_query = moved.reshape(held_rows, per_device, heads_dev, head_dim)
    key_value = jnp.stack([key_rows, value_rows]).reshape(
        2, row_count, 1, groups, per_device, width
    )
    key_value = jnp.broadcast_to(key_value, (2, row_count, copies, groups, per_device, width))
    key_value = key_value.reshape(2, row_count, ctx_count, per_device, width)
    held_keys = lax.all_to_all(key_value, "ctx", split_axis=2, concat_axis=1, tiled=True)
    key_pos = jnp.arange(ctx_count * row_count)
    result = phase_attend(phase_query, held_keys[0], held_keys[1], query_pos, key_pos, score_scale)
    outgoing = result.reshape(ctx_count, row_count // copies, 1, per_device, width)
    returned = lax.all_to_all(
        outgoing.astype(jnp.bfloat16), "ctx", split_axis=0, concat_axis=2, tiled=True
    ).astype(outgoing.dtype)
    return returned.reshape(tokens_dev, heads_dev, head_dim)


def summary_section(query, key_rows, value_rows, score_scale):
    tokens_dev, heads_dev, head_dim = query.shape
    width = heads_dev * head_dim
    local_blocks = tokens_dev // BLOCK
    picked = jnp.stack([key_rows, value_rows]).reshape(2, local_blocks, BLOCK, width)[
        :, :, BLOCK - SUMCOLS :
    ]
    picked = picked.reshape(2, local_blocks * SUMCOLS, width)
    gathered = lax.all_gather(picked, "ctx", axis=1, tiled=True)
    total_keys = gathered.shape[1]
    gathered = gathered.reshape(2, total_keys, heads_dev, head_dim)
    index = jnp.arange(total_keys)
    key_pos = index // SUMCOLS * BLOCK + BLOCK - SUMCOLS + index % SUMCOLS
    step_rows = min(tokens_dev, 512)
    count_blocks = tokens_dev // step_rows
    first = lax.axis_index("ctx") * tokens_dev

    def summary_one_block(operands):
        number, block_query, block_keys, block_values = operands
        local_pos = number * step_rows + jnp.arange(step_rows)
        query_pos = first + local_pos
        logit_scores = (
            jnp.einsum("qhd,khd->hqk", block_query, gathered[0], preferred_element_type=jnp.float32)
            * score_scale
        )
        permitted_mask = (key_pos[None, :] <= query_pos[:, None])[None]
        own_score = (
            jnp.sum(block_query.astype(jnp.float32) * block_keys.astype(jnp.float32), axis=-1).T
            * score_scale
        )
        own_allowed = (local_pos % BLOCK < BLOCK - SUMCOLS)[None]
        masked = jnp.where(permitted_mask, logit_scores, BIG_NEG)
        own_masked = jnp.where(own_allowed, own_score, BIG_NEG)
        row_top = jnp.maximum(jnp.max(masked, axis=-1), own_masked)
        exponent = jnp.where(permitted_mask, jnp.exp(masked - row_top[..., None]), 0.0)
        own_exponent = jnp.where(own_allowed, jnp.exp(own_masked - row_top), 0.0)
        total = jnp.sum(exponent, axis=-1) + own_exponent
        result = jnp.einsum(
            "hqk,khd->hqd",
            exponent.astype(jnp.bfloat16),
            gathered[1],
            preferred_element_type=jnp.float32,
        )
        own_rounded = lax.optimization_barrier(own_exponent.astype(jnp.bfloat16)).astype(
            jnp.float32
        )
        result = result + own_rounded[..., None] * jnp.transpose(block_values, (1, 0, 2)).astype(
            jnp.float32
        )
        return jnp.transpose(result / total[..., None], (1, 0, 2))

    result = lax.map(
        summary_one_block,
        (
            jnp.arange(count_blocks),
            query.reshape(count_blocks, step_rows, heads_dev, head_dim),
            key_rows.reshape(count_blocks, step_rows, heads_dev, head_dim),
            value_rows.reshape(count_blocks, step_rows, heads_dev, head_dim),
        ),
    )
    return result.reshape(tokens_dev, heads_dev, head_dim)


def body(queries, keys, values, out_weight):
    tokens_dev, width = queries.shape
    head_dim = HEAD_SIZE
    heads_dev = width // head_dim
    score_scale = head_dim ** (-0.5)
    query = queries.reshape(tokens_dev, heads_dev, head_dim)
    key_rows = keys.reshape(tokens_dev, heads_dev, head_dim)
    value_rows = values.reshape(tokens_dev, heads_dev, head_dim)
    local_out = local_section(query, key_rows, value_rows, score_scale)
    stride_out = stride_section(query, key_rows, value_rows, score_scale)
    summary_out = summary_section(query, key_rows, value_rows, score_scale)
    attended = (
        (local_out + stride_out + summary_out).astype(jnp.bfloat16).reshape(tokens_dev, width)
    )
    return lax.psum_scatter(
        jnp.dot(attended, out_weight, preferred_element_type=jnp.float32).astype(jnp.bfloat16),
        "head",
        scatter_dimension=0,
        tiled=True,
    )


def solution(mesh):
    placed = (P("ctx", "head"), P("ctx", "head"), P("ctx", "head"), P("head", None))
    return jax.shard_map(
        body, mesh=mesh, in_specs=placed, out_specs=P(("ctx", "head"), None), check_vma=False
    )
```

profile of v0, /device:TPU:3, one launch (start us, length us, event | category | flops | bytes accessed | tf_op | source)
XLA Modules:
  0.0 220.6 jit_solution(6892863146962862190)
XLA Ops:
  6.5 0.0 copy-start
  6.5 0.0 copy-start.3
  6.5 0.0 copy-start.1
  6.5 1.2 maximum_bitcast_fusion.4
  7.7 0.1 copy.39
  7.9 1.3 broadcast_in_dim.79
  9.2 13.7 %all-to-all-start.1 = ((bf16[2,64,32,1,128]{4,1,0,3,2:T(8,128)(2,1)}), bf16[2,64,32,1,128]{4,1,0,3,2:T(8,128)(2,1)S(1)}, u32[]{:S(2)}, u32[]{:S(2)}) async-start(bf16[2,64,32,1,128]{4,1,0,3,2:T(8,128)(2,1)} %bitcast.23), calls=%async_computation.1 | async-start | bytes 2097152 | tf_op jit(solution)/shard_map/all_to_all | solution.py:111
  22.9 0.0 all-gather.2.cloned.1.call-start
  23.0 0.0 copy-done.3
  23.0 0.0 copy-done.1
  23.0 0.6 fusion.94
  23.6 0.0 all-gather.2.cloned.1.call-update
  23.7 3.4 %collective-permute-start = (bf16[2,512,1,128]{3,1,2,0:T(8,128)(2,1)S(1)}, bf16[2,512,1,128]{3,1,2,0:T(8,128)(2,1)S(1)}, u32[]{:S(2)}, u32[]{:S(2)}) collective-permute-start(bf16[2,512,1,128]{3,1,2,0:T(8,128)(2,1)S(1)} %pad_maximum_fusion.2), channel_id=1, source_target_pairs={{0,16},{16,32},{32,48},{48,64},{64,80},{80,96},{96,112},{112,128},... | collective-permute-start | bytes 786440 | tf_op jit(solution)/shard_map/ppermute | solution.py:19
  27.2 0.1 add_compare_fusion
  27.3 0.1 iota_add_fusion.1
  27.3 0.0 copy-done.2
  27.3 0.8 copy.38
  28.2 0.1 iota_add_fusion.2
  28.2 5.3 %collective-permute-done = bf16[2,512,1,128]{3,1,2,0:T(8,128)(2,1)S(1)} collective-permute-done((bf16[2,512,1,128]{3,1,2,0:T(8,128)(2,1)S(1)}, bf16[2,512,1,128]{3,1,2,0:T(8,128)(2,1)S(1)}, u32[]{:S(2)}, u32[]{:S(2)}) %collective-permute-start) | collective-permute-done | bytes 262176 | tf_op jit(solution)/shard_map/ppermute | solution.py:19
  33.6 0.7 pad_maximum_fusion
  34.3 4.5 %fusion.105 = (f32[2,512]{1,0:T(2,128)S(1)}, bf16[2,512,1024]{1,2,0:T(8,128)(2,1)}) fusion(s32[2,512]{1,0:T(2,128)S(1)} %get-tuple-element.293, s32[2,512]{1,0:T(2,128)S(1)} %get-tuple-element.292, s32[2,1024]{1,0:T(2,128)S(1)} %iota_add_fusion.1, pred[2,1024]{1,0:T(4,128)(4,1)S(1)} %add_compare_fusion, bf16[2,512,128]{2,1,0:T(8,128)(2,1)S(1)} %bitcast.167, ...), kind=kOutput, calls=%fused_computation.136 | convolution fusion | flops 284165120 | bytes 2906112 | tf_op jit(solution)/shard_map/sub | solution.py:25
  38.8 6.5 %all-to-all-done.1 = bf16[2,64,32,1,128]{4,1,0,3,2:T(8,128)(2,1)S(1)} async-done(((bf16[2,64,32,1,128]{4,1,0,3,2:T(8,128)(2,1)}), bf16[2,64,32,1,128]{4,1,0,3,2:T(8,128)(2,1)S(1)}, u32[]{:S(2)}, u32[]{:S(2)}) %all-to-all-start.1) | async-done | bytes 1048608 | tf_op jit(solution)/shard_map/all_to_all | solution.py:111
  45.4 22.0 %all-to-all-start = ((bf16[1,32,32,1,128]{4,1,3,0,2:T(8,128)(2,1)}), bf16[1,32,32,1,128]{4,1,3,0,2:T(8,128)(2,1)}, u32[]{:S(2)}, u32[]{:S(2)}) async-start(bf16[1,32,32,1,128]{4,1,3,0,2:T(8,128)(2,1)} %copy.38), calls=%async_computation | async-start | bytes 524288 | tf_op jit(solution)/shard_map/all_to_all | solution.py:104
  67.4 2.6 %fusion.84 = f32[2,512,128]{2,1,0:T(8,128)S(1)} fusion(bf16[2,512,1024]{1,2,0:T(8,128)(2,1)} %get-tuple-element.295, bf16[2,512,1,128]{3,1,0,2:T(8,128)(2,1)S(1)} %bitcast.172, bf16[2,512,1,128]{3,1,0,2:T(8,128)(2,1)} %bitcast.178, f32[2,512]{1,0:T(2,128)S(1)} %get-tuple-element.294), kind=kOutput, calls=%fused_computation.93 | convolution fusion | flops 269615104 | bytes 3149824 | tf_op jit(solution)/shard_map/bhqk,bkhd->bhqd/dot_general | solution.py:27
  70.0 0.1 copy.50
  70.1 0.1 fusion.104
  70.2 9.8 %all-to-all-done = bf16[1,32,32,1,128]{4,1,3,0,2:T(8,128)(2,1)} async-done(((bf16[1,32,32,1,128]{4,1,3,0,2:T(8,128)(2,1)}), bf16[1,32,32,1,128]{4,1,3,0,2:T(8,128)(2,1)}, u32[]{:S(2)}, u32[]{:S(2)}) %all-to-all-start) | async-done | bytes 262176 | tf_op jit(solution)/shard_map/all_to_all | solution.py:104
  80.0 10.5 %while.24 = (s32[]{:T(128)}, bf16[2,512,1,1,128]{4,1,3,2,0:T(8,128)(2,1)}, s32[2,512]{1,0:T(2,128)S(1)}, bf16[2,512,1,1,128]{4,1,3,2,0:T(8,128)(2,1)}, bf16[2048...) while((s32[]{:T(128)}, ...), condition=%wide.region_5.6_spmd.clone, body=%wide.region_2.5_spmd.clone.sunk | while | flops 553712640 | bytes 16142489 | solution.py:85
  80.0 1.9 fusion.125
  81.9 1.4 fusion.126
  83.3 0.0 copy-done.4
  83.3 1.3 fusion.127
  84.6 0.0 copy-start.5
  84.6 0.7 copy-done.5
  85.3 1.9 fusion.125
  87.2 1.4 fusion.126
  88.5 0.0 copy-done.4
  88.5 1.3 fusion.127
  89.8 0.7 copy-done.5
  90.5 4.6 %all-to-all-start.2 = ((bf16[32,32,1,1,128]{4,1,3,2,0:T(8,128)(2,1)}), bf16[32,32,1,1,128]{4,1,3,2,0:T(8,128)(2,1)S(1)}, u32[]{:S(2)}, u32[]{:S(2)}) async-start(bf16[32,32,1,1,128]{4,1,3,2,0:T(8,128)(2,1)} %bitcast.177), calls=%async_computation.2 | async-start | bytes 524288 | tf_op jit(solution)/shard_map/all_to_all | solution.py:115
  95.1 0.2 reduce-scatter.2.cloned.1.call-start
  95.3 0.0 all-gather.2.cloned.1.call-done
  95.4 11.9 %while.25 = (s32[]{:T(128)}, f32[2,512,1,128]{3,1,2,0:T(8,128)S(1)}, s32[]{:T(128)}, s32[2]{0:T(128)S(1)}, bf16[2,512,1,128]{3,1,2,0:T(8,128)(2,1)S(1)}, /*index...) while((s32[]{:T(128)}, ...), condition=%wide.region_10.11_spmd.clone, body=%wide.region_6.10_spmd.clone.sunk | while | flops 554230272 | bytes 18692288 | solution.py:172
  95.4 0.6 dynamic_slice.69
  96.6 0.0 copy-start.6
  96.6 2.1 fusion.132
  98.6 0.2 multiply_reduce_fusion.2
  98.8 1.2 fusion.133
  100.1 0.0 copy-done.6
  100.1 1.2 fusion.135
  101.3 0.6 dynamic_slice.69
  102.5 0.0 copy-start.6
  102.5 2.1 fusion.132
  104.6 0.2 multiply_reduce_fusion.2
  104.8 1.2 fusion.133
  106.1 0.0 copy-done.6
  106.1 1.2 fusion.135
  107.3 0.6 all-to-all-done.2
  107.8 0.1 bitcast_convert_fusion
  107.9 0.1 fusion.93
  108.0 0.0 copy-done
  108.0 3.2 %convolution_convert_fusion = bf16[1024,2048]{1,0:T(8,128)(2,1)} fusion(bf16[1024,128]{1,0:T(8,128)(2,1)S(1)} %fusion.93, bf16[128,2048]{1,0:T(8,128)(2,1)S(1)} %copy-done), kind=kOutput, calls=%fused_computation.83 | convolution fusion | flops 538968064 | bytes 4980736 | tf_op jit(solution)/shard_map/dot_general | solution.py:199
  111.2 0.0 reduce-scatter.2.cloned.1.call-update
  111.2 102.5 %reduce-scatter.2.cloned.1.call-done = bf16[64,2048]{1,0:T(8,128)(2,1)} async-done(((bf16[1024,2048]{1,0:T(8,128)(2,1)}), bf16[64,2048]{1,0:T(8,128)(2,1)}) %reduce-scatter.2.cloned.1.call-update) | async-done | bytes 262160 | tf_op jit(solution)/shard_map/reduce_scatter | solution.py:198
  (28 shorter events, 0.3 us)
Async XLA Ops:
  6.5 101.5 %copy-start = (bf16[128,2048]{1,0:T(8,128)(2,1)S(1)}, bf16[128,2048]{1,0:T(8,128)(2,1)}, u32[]{:S(2)}) copy-start(bf16[128,2048]{1,0:T(8,128)(2,1)} %param.11) | copy-start | bytes 1572868
  6.5 16.5 %copy-start.3 = (bf16[1024,128]{1,0:T(8,128)(2,1)S(1)}, bf16[1024,128]{1,0:T(8,128)(2,1)}, u32[]{:S(2)}) copy-start(bf16[1024,128]{1,0:T(8,128)(2,1)} %param.10) | copy-start | bytes 786436
  6.5 16.5 %copy-start.1 = (bf16[1024,128]{1,0:T(8,128)(2,1)S(1)}, bf16[1024,128]{1,0:T(8,128)(2,1)}, u32[]{:S(2)}) copy-start(bf16[1024,128]{1,0:T(8,128)(2,1)} %param.9) | copy-start | bytes 786436
  6.5 20.8 %copy-start.2 = (bf16[1024,128]{1,0:T(8,128)(2,1)S(1)}, bf16[1024,128]{1,0:T(8,128)(2,1)}, u32[]{:S(2)}) copy-start(bf16[1024,128]{1,0:T(8,128)(2,1)} %param.8) | copy-start | bytes 786436
  9.2 36.2 %all-to-all-start.1 = ((bf16[2,64,32,1,128]{4,1,0,3,2:T(8,128)(2,1)}), bf16[2,64,32,1,128]{4,1,0,3,2:T(8,128)(2,1)S(1)}, u32[]{:S(2)}, u32[]{:S(2)}) async-start(bf16[2,64,32,1,128]{4,1,0,3,2:T(8,128)(2,1)} %bitcast.23), calls=%async_computation.1 | async-start | bytes 2097152 | tf_op jit(solution)/shard_map/all_to_all | solution.py:111
  22.9 72.4 %all-gather.2.cloned.1.call-start = ((), (), s32[]{:S(2)}) async-start(), calls=%async_computation.4 | async-start | bytes 1081344 | tf_op jit(solution)/shard_map/all_gather | solution.py:129
  23.7 9.8 %collective-permute-start = (bf16[2,512,1,128]{3,1,2,0:T(8,128)(2,1)S(1)}, bf16[2,512,1,128]{3,1,2,0:T(8,128)(2,1)S(1)}, u32[]{:S(2)}, u32[]{:S(2)}) collective-permute-start(bf16[2,512,1,128]{3,1,2,0:T(8,128)(2,1)S(1)} %pad_maximum_fusion.2), channel_id=1, source_target_pairs={{0,16},{16,32},{32,48},{48,64},{64,80},{80,96},{96,112},{112,128},... | collective-permute-start | bytes 786440 | tf_op jit(solution)/shard_map/ppermute | solution.py:19
  45.4 34.6 %all-to-all-start = ((bf16[1,32,32,1,128]{4,1,3,0,2:T(8,128)(2,1)}), bf16[1,32,32,1,128]{4,1,3,0,2:T(8,128)(2,1)}, u32[]{:S(2)}, u32[]{:S(2)}) async-start(bf16[1,32,32,1,128]{4,1,3,0,2:T(8,128)(2,1)} %copy.38), calls=%async_computation | async-start | bytes 524288 | tf_op jit(solution)/shard_map/all_to_all | solution.py:104
  80.0 3.3 %copy-start.4 = (bf16[2,512,1,1,128]{4,1,3,2,0:T(8,128)(2,1)S(1)}, bf16[2,512,1,1,128]{4,1,3,2,0:T(8,128)(2,1)}, u32[]{:S(2)}) copy-start(bf16[2,512,1,1,128]{4,1,3,2,0:T(8,128)(2,1)} %get-tuple-element.406) | copy-start | bytes 786436 | tf_op jit(solution)/shard_map/while
  84.6 0.7 copy-start.5
  85.3 3.3 %copy-start.4 = (bf16[2,512,1,1,128]{4,1,3,2,0:T(8,128)(2,1)S(1)}, bf16[2,512,1,1,128]{4,1,3,2,0:T(8,128)(2,1)}, u32[]{:S(2)}) copy-start(bf16[2,512,1,1,128]{4,1,3,2,0:T(8,128)(2,1)} %get-tuple-element.406) | copy-start | bytes 786436 | tf_op jit(solution)/shard_map/while
  89.8 0.7 copy-start.5
  90.5 17.3 %all-to-all-start.2 = ((bf16[32,32,1,1,128]{4,1,3,2,0:T(8,128)(2,1)}), bf16[32,32,1,1,128]{4,1,3,2,0:T(8,128)(2,1)S(1)}, u32[]{:S(2)}, u32[]{:S(2)}) async-start(bf16[32,32,1,1,128]{4,1,3,2,0:T(8,128)(2,1)} %bitcast.177), calls=%async_computation.2 | async-start | bytes 524288 | tf_op jit(solution)/shard_map/all_to_all | solution.py:115
  95.1 118.6 %reduce-scatter.2.cloned.1.call-start = ((), (), s32[]{:S(2)}) async-start(), calls=%async_computation.5 | async-start | bytes 4456448 | tf_op jit(solution)/shard_map/reduce_scatter | solution.py:198
  96.6 3.6 %copy-start.6 = (bf16[2,2048,1,128]{3,1,2,0:T(8,128)(2,1)S(1)}, bf16[2,2048,1,128]{3,1,2,0:T(8,128)(2,1)}, u32[]{:S(2)}) copy-start(bf16[2,2048,1,128]{3,1,2,0:T(8,128)(2,1)} %get-tuple-element.444) | copy-start | bytes 3145732 | tf_op jit(solution)/shard_map/while
  102.5 3.6 %copy-start.6 = (bf16[2,2048,1,128]{3,1,2,0:T(8,128)(2,1)S(1)}, bf16[2,2048,1,128]{3,1,2,0:T(8,128)(2,1)}, u32[]{:S(2)}) copy-start(bf16[2,2048,1,128]{3,1,2,0:T(8,128)(2,1)} %get-tuple-element.444) | copy-start | bytes 3145732 | tf_op jit(solution)/shard_map/while
Sparse Core Ops, SparseCore 0:
  26.9 63.0 all-gather.1
  111.4 102.3 reduce-scatter.1
where the time goes:
time: 224 us; the launch traced here: 221 us
  waiting for transfers between devices  125 us (56%)
  starting transfers between devices  44 us (20%)
  matrix products  23.2 us (10%)
  between operations  13.6 us (6%)
  other arithmetic  8.7 us (4%)
  local copies, waits for them, and re-layouts  5.08 us (2%)
    reduce_scatter x1, waiting for transfers between devices, body(): lax.psum_scatter(jnp.dot(attended, out_weight, preferred_element_type=jnp...  102 us
    all_to_all x1, starting transfers between devices, stride_section(): lax.all_to_all(shaped, 'ctx', split_axis=2, concat_axis=1, tiled=True)  22 us
    all_to_all x1, starting transfers between devices, stride_section(): lax.all_to_all(key_value, 'ctx', split_axis=2, concat_axis=1, tiled=True)  13.7 us
    all_to_all x1, waiting for transfers between devices, stride_section(): lax.all_to_all(shaped, 'ctx', split_axis=2, concat_axis=1, tiled=True)  9.82 us
    all_to_all x1, waiting for transfers between devices, stride_section(): lax.all_to_all(key_value, 'ctx', split_axis=2, concat_axis=1, tiled=True)  6.53 us
    ppermute x1, waiting for transfers between devices, from_behind(): lax.ppermute(value, axis, [(source, source + steps) for source in range(i...  5.29 us
    dot_general x3, matrix products, softmax_weighted(): jnp.einsum(form, exponent.astype(jnp.bfloat16), value_rows, preferred_ele...  5.17 us
    all_to_all x1, starting transfers between devices, stride_section(): lax.all_to_all(outgoing.astype(jnp.bfloat16), 'ctx', split_axis=0, concat...  4.57 us
  transfers between devices with their start and end apart: 6, of which 5 were waited for; matrix products, arithmetic and copies ran while one was open for 13% of the time, Pallas kernels for 0%

commit v1 on v0

v1 whole, which is shorter than its diff:
```python
import functools
import math

import jax
import jax.numpy as jnp
from jax import lax
from jax.experimental import pallas as pl
from jax.experimental.pallas import tpu as pltpu
from jax.sharding import PartitionSpec as P

MESH = pl.DeviceIdType.MESH
NEG = -1e30
HEAD_SIZE = 128
WINDOW = 512
LOGIT = math.log2(math.e) * HEAD_SIZE ** -0.5
F32 = jnp.float32
BF16 = jnp.bfloat16
TOKENS = 1024
CHIPS = 16
ROWS = 64
LT = 256
SPAN = LT + WINDOW


def scores(q, k):
    return lax.dot_general(q, k, (((1,), (1,)), ((), ())), preferred_element_type=F32)


def mix(p, v):
    return jnp.dot(p.astype(BF16), v, preferred_element_type=F32)


def fold(q, k, v, state, allowed=None):
    top, total, acc = state
    s = scores(q, k)
    if allowed is not None:
        s = jnp.where(allowed, s, NEG)
    new_top = jnp.maximum(top, jnp.max(s, axis=-1, keepdims=True))
    p = jnp.exp2((s - new_top) * LOGIT)
    shrink = jnp.exp2((top - new_top) * LOGIT)
    total = shrink * total + jnp.sum(p, axis=-1, keepdims=True)
    acc = shrink * acc + mix(p, v)
    return new_top, total, acc


def iota(shape, dim):
    return lax.broadcasted_iota(jnp.int32, shape, dim)


def kernel(
    q_hbm, k_hbm, v_hbm, w_hbm, out_ref,
    q, kv, stage, rq, rkv, own_sum, summ, ls, ret_out, ret, att_out, att, wbuf,
    in_sem, bar_unused, halo_sem, q_send, q_recv, kv_send, kv_recv, pair_send, pair_recv,
    sz_send, sz_recv, sx_send, sx_recv, sp_send, sp_recv,
    wz_sem, wy_send, wy_recv, wp_send, wp_recv,
    r_send, r_recv, a_send, a_recv,
):
    c = lax.axis_index("ctx")
    h = lax.axis_index("head")
    core, x, zh = c % 2, (c // 2) % 4, c // 8
    zl, y = h % 2, h // 2
    chip = zh * 4 + x
    sib = c + 1 - 2 * core
    sends = []

    def remote(src, dst, ssem, rsem, dev):
        return pltpu.make_async_remote_copy(
            src_ref=src, dst_ref=dst, send_sem=ssem, recv_sem=rsem,
            device_id=dev, device_id_type=MESH,
        )

    def go(copy):
        copy.start()
        sends.append(copy)
        return copy

    def chip_at(dz, dx):
        return ((zh + dz) % 4) * 4 + (x + dx) % 4

    offs = [(dz, dx) for dz in (2, 1, 3, 0) for dx in (2, 1, 3, 0) if dz or dx]
    heads = [(dy, dz) for dy in (4, 3, 5, 2, 6, 1, 7, 0) for dz in (1, 0) if dy or dz]

    loads = [
        pltpu.make_async_copy(q_hbm, q, in_sem.at[0]),
        pltpu.make_async_copy(k_hbm, kv.at[0, pl.ds(WINDOW, TOKENS)], in_sem.at[1]),
        pltpu.make_async_copy(v_hbm, kv.at[1, pl.ds(WINDOW, TOKENS)], in_sem.at[2]),
        pltpu.make_async_copy(w_hbm, wbuf.at[h], in_sem.at[3]),
    ]
    for load in loads:
        load.start()

    barrier = pltpu.get_barrier_semaphore()

    def greet(dev):
        pl.semaphore_signal(barrier, inc=1, device_id=dev, device_id_type=MESH)

    for dz, dx in offs:
        greet((chip_at(dz, dx) * 2 + core, h))
    for dy, dz in heads:
        greet((c, ((y + dy) % 8) * 2 + (zl + dz) % 2))
    greet((sib, h))
    greet(((c + 2 * core - 1) % 32, h))

    for load in loads[:3]:
        load.wait()

    ri, ci = iota((256, 256), 0), iota((256, 256), 1)
    swap = jnp.where(((ri >> 4) == (ci & 15)) & ((ri & 15) == (ci >> 4)), 1.0, 0.0).astype(BF16)
    for n in range(3):
        for b in range(4):
            if n == 0:
                rows = q[pl.ds(256 * b, 256), :]
            else:
                rows = kv[n - 1, pl.ds(WINDOW + 256 * b, 256), :]
            moved = jnp.dot(swap, rows, preferred_element_type=F32).astype(BF16)
            stage[:, n, pl.ds(16 * b, 16), :] = moved.reshape(CHIPS, 16, HEAD_SIZE)
    for n in range(2):
        parts = [
            kv[n, pl.ds(WINDOW + 128 * g + 112, 16), :].astype(F32)[8:] for g in range(8)
        ]
        own_sum[n] = jnp.concatenate(parts, axis=0).astype(BF16)

    rr, cc = iota((LT, SPAN), 0), iota((LT, SPAN), 1)

    def local_tile(i, bias):
        qs = q[pl.ds(pl.multiple_of(i * LT, LT), LT), :]
        window = pl.ds(pl.multiple_of(i * LT, LT), SPAN)
        s = scores(qs, kv[0, window, :])
        allowed = (cc > rr) & (cc <= rr + WINDOW)
        if bias:
            start = jnp.where(c == 0, WINDOW - i * LT, 0)
            allowed = allowed & (cc >= start)
        s = jnp.where(allowed, s, NEG)
        top = jnp.max(s, axis=-1, keepdims=True)
        p = jnp.exp2((s - top) * LOGIT)
        total = jnp.sum(p, axis=-1, keepdims=True)
        ls[pl.ds(pl.multiple_of(i * LT, LT), LT), :] = mix(p, kv[1, window, :]) / total

    half = WINDOW // LT

    @pl.loop(half, TOKENS // LT)
    def _(i):
        local_tile(i, False)

    pl.semaphore_wait(barrier, 32)

    def w_unit(yy, zz, k):
        return wbuf.at[2 * (yy % 8) + zz % 2, pl.ds(pl.multiple_of(64 * k, 64), 64), :]

    for n, dz in enumerate((2, 1, 3)):
        dev = (((zh + dz) % 4) * 8 + x * 2 + core, h)
        go(remote(own_sum, summ.at[:, zh, x, core], sz_send.at[n], sz_recv.at[n], dev))
    loads[3].wait()
    zpeer = (c, 2 * y + 1 - zl)
    go(remote(w_unit(y, zl, core), w_unit(y, zl, core), wz_sem.at[0], wz_sem.at[1], zpeer))

    def w_dev(d):
        return (c, 2 * ((y + (1, -1)[d]) % 8) + zl)

    def w_name(d, i):
        step = i // 2
        kind = (zl, 1 - zl)[i % 2] if i < 6 else (zl, 1 - zl)[d]
        return (y - (1, -1)[d] * step + 8, kind)

    def w_send(d, i):
        yy, zz = w_name(d, i)
        ref = w_unit(yy, zz, core)
        go(remote(ref, ref, wy_send.at[d, i], wy_recv.at[d, i], w_dev(d)))

    def w_pair(yy, zz, n):
        ref = w_unit(yy, zz, core)
        go(remote(ref, ref, wp_send.at[n], wp_recv.at[n], (sib, h)))

    def w_wait(d, i):
        yy, zz = w_name(d, i)
        yy = yy - (1, -1)[d]
        ref = w_unit(yy + 8, zz, core)
        remote(ref, ref, wy_send.at[d, i], wy_recv.at[d, i], w_dev(d)).wait_recv()
        return yy + 8, zz

    def w_relay(i):
        for d in range(2):
            yy, zz = w_wait(d, i)
            if i < 4:
                w_send(d, i + 2)
            elif i == 4 and d == 0 or i == 5 and d == 1:
                w_send(d, 6)
            w_pair(yy, zz, 1 + 7 * d + i)

    w_send(0, 0)
    w_send(1, 0)
    next_dev = ((c + 1) % 32, h)
    go(remote(
        kv.at[:, pl.ds(TOKENS, WINDOW)], kv.at[:, pl.ds(0, WINDOW)],
        halo_sem.at[0], halo_sem.at[1], next_dev,
    ))
    for n, (dz, dx) in enumerate(offs):
        to = chip_at(dz, dx)
        go(remote(stage.at[to, pl.ds(1, 2)], rkv.at[:, chip, core], kv_send.at[n], kv_recv.at[n], (to * 2 + core, h)))
    for n, (dz, dx) in enumerate(offs):
        to = chip_at(dz, dx)
        go(remote(stage.at[to, 0], rq.at[chip], q_send.at[n], q_recv.at[n], (to * 2 + core, h)))
    own = [
        pltpu.make_async_copy(stage.at[chip, pl.ds(1, 2)], rkv.at[:, chip, core], in_sem.at[4]),
        pltpu.make_async_copy(stage.at[chip, 0], rq.at[chip], in_sem.at[5]),
        pltpu.make_async_copy(own_sum, summ.at[:, zh, x, core], in_sem.at[6]),
    ]
    for copy in own:
        copy.start()
    go(remote(stage.at[chip, pl.ds(1, 2)], rkv.at[:, chip, core], pair_send.at[15], pair_recv.at[15], (sib, h)))

    remote(
        kv.at[:, pl.ds(TOKENS, WINDOW)], kv.at[:, pl.ds(0, WINDOW)],
        halo_sem.at[0], halo_sem.at[1], next_dev,
    ).wait_recv()

    @pl.loop(0, half)
    def _(i):
        local_tile(i, True)

    own[2].wait()
    for n, dz in enumerate((2, 1, 3)):
        ref = summ.at[:, (zh - dz + 4) % 4, x, core]
        remote(own_sum, ref, sz_send.at[n], sz_recv.at[n], (c, h)).wait_recv()
    for n, dx in enumerate((2, 1, 3)):
        dev = (zh * 8 + ((x + dx) % 4) * 2 + core, h)
        ref = summ.at[:, :, x, core]
        go(remote(ref, ref, sx_send.at[n], sx_recv.at[n], dev))
    ref = summ.at[:, :, x, core]
    go(remote(ref, ref, sp_send.at[3], sp_recv.at[3], (sib, h)))

    ref = w_unit(y, 1 - zl, core)
    remote(ref, ref, wz_sem.at[0], wz_sem.at[1], zpeer).wait_recv()
    w_send(0, 1)
    w_send(1, 1)
    w_pair(y, 1 - zl, 0)

    for n, dx in enumerate((2, 1, 3)):
        ref = summ.at[:, :, (x - dx + 4) % 4, core]
        remote(ref, ref, sx_send.at[n], sx_recv.at[n], (c, h)).wait_recv()
        go(remote(ref, ref, sp_send.at[n], sp_recv.at[n], (sib, h)))
    for n, dx in enumerate((2, 1, 3, 0)):
        ref = summ.at[:, :, (x - dx + 4) % 4, 1 - core]
        remote(ref, ref, sp_send.at[n], sp_recv.at[n], (sib, h)).wait_recv()

    def take_pairs(part):
        for n in part:
            dz, dx = offs[n]
            ref = rkv.at[:, ((zh - dz + 4) % 4) * 4 + (x - dx + 4) % 4, core]
            remote(ref, ref, kv_send.at[n], kv_recv.at[n], (c, h)).wait_recv()
            go(remote(ref, ref, pair_send.at[n], pair_recv.at[n], (sib, h)))

    qrow = iota((256, 512), 0)
    kcol = iota((256, 512), 1)

    def summary_tile(i):
        rows = pl.ds(pl.multiple_of(i * 256, 256), 256)
        qs = q[rows, :]
        own_rows = pl.ds(pl.multiple_of(WINDOW + i * 256, 256), 256)
        ks = kv[0, own_rows, :].astype(F32)
        vs = kv[1, own_rows, :].astype(F32)
        self_score = jnp.sum(qs.astype(F32) * ks, axis=-1, keepdims=True)
        apart = (iota((256, 1), 0) & 127) < 120
        state = (
            jnp.where(apart, self_score, NEG),
            jnp.where(apart, 1.0, 0.0),
            jnp.where(apart, vs, 0.0),
        )

        def step(t, state):
            return fold(
                qs, summ[0, t].reshape(512, HEAD_SIZE), summ[1, t].reshape(512, HEAD_SIZE), state
            )

        state = lax.fori_loop(0, zh, step, state)
        at = qrow + (i * 256 + (2 * x + core) * TOKENS)
        key_at = (kcol >> 3) * 128 + 120 + (kcol & 7)
        state = fold(
            qs, summ[0, zh].reshape(512, HEAD_SIZE), summ[1, zh].reshape(512, HEAD_SIZE),
            state, key_at <= at,
        )
        ls[rows, :] = ls[rows, :] + state[2] / state[1]

    @pl.loop(0, 2)
    def _(i):
        summary_tile(i)

    w_relay(0)
    take_pairs(range(0, 8))

    @pl.loop(2, 4)
    def _(i):
        summary_tile(i)

    w_relay(1)
    take_pairs(range(8, 15))
    own[0].wait()
    own[1].wait()
    for n in range(15):
        dz, dx = offs[n]
        src = ((zh - dz + 4) % 4) * 4 + (x - dx + 4) % 4
        remote(rq.at[src], rq.at[src], q_send.at[n], q_recv.at[n], (c, h)).wait_recv()
        ref = rkv.at[:, src, 1 - core]
        remote(ref, ref, pair_send.at[n], pair_recv.at[n], (sib, h)).wait_recv()
    ref = rkv.at[:, chip, 1 - core]
    remote(ref, ref, pair_send.at[15], pair_recv.at[15], (sib, h)).wait_recv()

    nrow = iota((256, 512), 0)
    order = (nrow >> 6) * 128 + core * 64 + (nrow & 63)

    def stride_tile(n, dz):
        b = (zh + dz) % 4
        qs = rq[pl.ds(b * 4, 4)].reshape(256, HEAD_SIZE)

        def keys(t):
            return (
                rkv[0, pl.ds(t * 4, 4)].reshape(512, HEAD_SIZE),
                rkv[1, pl.ds(t * 4, 4)].reshape(512, HEAD_SIZE),
            )

        def step(t, state):
            return fold(qs, *keys(t), state)

        state = (
            jnp.full((256, 1), NEG, F32), jnp.zeros((256, 1), F32),
            jnp.zeros((256, HEAD_SIZE), F32),
        )
        state = lax.fori_loop(0, b, step, state)
        state = fold(qs, *keys(b), state, kcol <= order)
        ret_out[n] = (state[2] / state[1]).astype(BF16).reshape(4, ROWS, HEAD_SIZE)

    back = [(n, dz, dx) for n, dz in enumerate((2, 1, 3, 0)) for dx in (2, 1, 3, 0)]

    def send_back(n, dz):
        for m, (nn, _, dx) in enumerate(back):
            if nn != n or not (dz or dx):
                continue
            to = chip_at(dz, dx)
            go(remote(
                ret_out.at[n, (x + dx) % 4], ret.at[chip], r_send.at[m], r_recv.at[m],
                (to * 2 + core, h),
            ))

    for n, dz in enumerate((2, 1, 3, 0)):
        stride_tile(n, dz)
        send_back(n, dz)
        if n == 1:
            w_relay(2)
    mine = pltpu.make_async_copy(ret_out.at[3, x], ret.at[chip], in_sem.at[7])
    mine.start()
    w_relay(3)
    mine.wait()
    for m, (n, dz, dx) in enumerate(back):
        if dz or dx:
            src = ((zh - dz + 4) % 4) * 4 + (x - dx + 4) % 4
            remote(ret.at[src], ret.at[src], r_send.at[m], r_recv.at[m], (c, h)).wait_recv()
    for b in range(4):
        rows = ret[:, pl.ds(16 * b, 16), :].reshape(256, HEAD_SIZE)
        back_rows = jnp.dot(swap, rows, preferred_element_type=F32)
        att_out[pl.ds(256 * b, 256), :] = (ls[pl.ds(256 * b, 256), :] + back_rows).astype(BF16)
    for n, (dy, dz) in enumerate(heads):
        to = ((y + dy) % 8) * 2 + (zl + dz) % 2
        go(remote(
            att_out.at[pl.ds(pl.multiple_of(to * 64, 64), 64)], att.at[h],
            a_send.at[n], a_recv.at[n], (c, to),
        ))
    mine = pltpu.make_async_copy(
        att_out.at[pl.ds(pl.multiple_of(h * 64, 64), 64)], att.at[h], in_sem.at[8]
    )
    mine.start()
    w_relay(4)
    w_relay(5)
    w_relay(6)
    mine.wait()
    for n, (dy, dz) in enumerate(heads):
        src = ((y - dy + 8) % 8) * 2 + (zl + dz) % 2
        remote(att.at[src], att.at[src], a_send.at[n], a_recv.at[n], (c, h)).wait_recv()
    ref = w_unit(y, 1 - zl, 1 - core)
    remote(ref, ref, wp_send.at[0], wp_recv.at[0], (sib, h)).wait_recv()
    for d in range(2):
        for i in range(7):
            yy, zz = w_name(d, i)
            ref = w_unit(yy - (1, -1)[d] + 8, zz, 1 - core)
            n = 1 + 7 * d + i
            remote(ref, ref, wp_send.at[n], wp_recv.at[n], (sib, h)).wait_recv()

    rows = jnp.concatenate([att[i] for i in range(16)], axis=-1)

    @pl.loop(0, 4)
    def _(n):
        cols = pl.ds(pl.multiple_of(n * 512, 512), 512)
        weights = wbuf[:, :, cols].reshape(2048, 512)
        out_ref[:, cols] = jnp.dot(rows, weights, preferred_element_type=F32).astype(BF16)

    for copy in sends:
        copy.wait_send()


def body(queries, keys, values, out_weight):
    dma = pltpu.SemaphoreType.DMA
    return pl.pallas_call(
        kernel,
        out_shape=jax.ShapeDtypeStruct((64, 2048), BF16),
        in_specs=[pl.BlockSpec(memory_space=pl.ANY)] * 4,
        out_specs=pl.BlockSpec(memory_space=pltpu.VMEM),
        scratch_shapes=[
            pltpu.VMEM((TOKENS, HEAD_SIZE), BF16),
            pltpu.VMEM((2, WINDOW + TOKENS, HEAD_SIZE), BF16),
            pltpu.VMEM((CHIPS, 3, ROWS, HEAD_SIZE), BF16),
            pltpu.VMEM((CHIPS, ROWS, HEAD_SIZE), BF16),
            pltpu.VMEM((2, CHIPS, 2, ROWS, HEAD_SIZE), BF16),
            pltpu.VMEM((2, ROWS, HEAD_SIZE), BF16),
            pltpu.VMEM((2, 4, 4, 2, ROWS, HEAD_SIZE), BF16),
            pltpu.VMEM((TOKENS, HEAD_SIZE), F32),
            pltpu.VMEM((4, 4, ROWS, HEAD_SIZE), BF16),
            pltpu.VMEM((CHIPS, ROWS, HEAD_SIZE), BF16),
            pltpu.VMEM((TOKENS, HEAD_SIZE), BF16),
            pltpu.VMEM((16, 64, HEAD_SIZE), BF16),
            pltpu.VMEM((16, HEAD_SIZE, 2048), BF16),
            dma((9,)), pltpu.SemaphoreType.REGULAR, dma((2,)),
            dma((15,)), dma((15,)), dma((15,)), dma((15,)), dma((16,)), dma((16,)),
            dma((3,)), dma((3,)), dma((3,)), dma((3,)), dma((4,)), dma((4,)),
            dma((2,)), dma((2, 7)), dma((2, 7)), dma((15,)), dma((15,)),
            dma((16,)), dma((16,)), dma((15,)), dma((15,)),
        ],
        compiler_params=pltpu.CompilerParams(collective_id=0, has_side_effects=True),
    )(queries, keys, values, out_weight)


def solution(mesh):
    placed = (P("ctx", "head"), P("ctx", "head"), P("ctx", "head"), P("head", None))
    return jax.shard_map(
        body, mesh=mesh, in_specs=placed, out_specs=P(("ctx", "head"), None), check_vma=False
    )
```

time: 224 us -> 92.1 us (0.41); the launches traced: 221 us -> 92 us
  waiting for transfers between devices: 125 us -> 0 us
  Pallas kernels: 0 us -> 90.3 us
  starting transfers between devices: 44 us -> 0 us
  matrix products: 23.2 us -> 0 us
  between operations: 13.6 us -> 0.01 us
  other arithmetic: 8.7 us -> 0 us
  local copies, waits for them, and re-layouts: 5.08 us -> 1.67 us
    reduce_scatter x1 -> x0, waiting for transfers between devices: 102 us -> none  [body(): lax.psum_scatter(jnp.dot(attended, out_weight, preferred_element_type=jnp...]
    pallas_call x0 -> x1, Pallas kernels: none -> 90.3 us  [body(): pl.pallas_call(kernel, out_shape=jax.ShapeDtypeStruct((64, 2048), BF16),...]
    all_to_all x3 -> x0, starting transfers between devices: 40.3 us -> none  [the longest x1 22 us: stride_section(): lax.all_to_all(shaped, 'ctx', split_axis=2, concat_axis=1, tiled=True)]
    dot_general x10 -> x0, matrix products: 18.6 us -> none  [the longest x3 5.17 us: softmax_weighted(): jnp.einsum(form, exponent.astype(jnp.bfloat16), value_rows, preferred_ele...]
    all_to_all x3 -> x0, waiting for transfers between devices: 16.9 us -> none  [the longest x1 9.82 us: stride_section(): lax.all_to_all(shaped, 'ctx', split_axis=2, concat_axis=1, tiled=True)]
    reduce_sum x6 -> x0, other arithmetic: 5.52 us -> none  [the longest x2 2.73 us: softmax_weighted(): total = jnp.sum(exponent, axis=-1, keepdims=True)]
    ppermute x1 -> x0, waiting for transfers between devices: 5.29 us -> none  [from_behind(): lax.ppermute(value, axis, [(source, source + steps) for source in range(i...]
    sub x1 -> x0, matrix products: 4.54 us -> none  [softmax_weighted(): exponent = jnp.where(permitted_mask, jnp.exp(masked - row_top), 0.0)]
  transfers between devices with their start and end apart: 6 -> 0, of which waited for: 5 -> 0; matrix products, arithmetic and copies ran while one was open for 13% -> 0% of each run, Pallas kernels for 0% -> 0%
where the time goes in v1:
time: 92.1 us; the launch traced here: 92 us
  Pallas kernels  90.3 us (98%)
  local copies, waits for them, and re-layouts  1.67 us (2%)
    pallas_call x1, Pallas kernels, body(): pl.pallas_call(kernel, out_shape=jax.ShapeDtypeStruct((64, 2048), BF16),...  90.3 us

profile of v1, /device:TPU:3, one launch (start us, length us, event | category | flops | bytes accessed | tf_op | source)
XLA Modules:
  0.0 92.0 jit_solution(10955062860415271651)
XLA Ops:
  0.0 90.3 %shard_map.46 = bf16[64,2048]{1,0:T(8,128)(2,1)} custom-call(bf16[1024,128]{1,0:T(8,128)(2,1)} %q_hbm.1, bf16[1024,128]{1,0:T(8,128)(2,1)} %k_hbm.1, bf16[1024,128]{1,0:T(8,128)(2,1)} %v_hbm.1, bf16[128,2048]{1,0:T(8,128)(2,1)} %w_hbm.1), custom_call_target="tpu_custom_call" | custom-call | tf_op jit(solution)/shard_map/pallas_call | solution.py:401
  90.3 1.7 %copy.6 = bf16[64,2048]{1,0:T(8,128)(2,1)} copy(bf16[64,2048]{1,0:T(8,128)(2,1)} %shard_map.46) | data formatting | bytes 524288

commit v2 on v1

v2 whole, which is shorter than its diff:
```python
import functools
import math

import jax
import jax.numpy as jnp
from jax import lax
from jax.experimental import pallas as pl
from jax.experimental.pallas import tpu as pltpu
from jax.sharding import PartitionSpec as P

MESH = pl.DeviceIdType.MESH
NEG = -1e30
HEAD_SIZE = 128
WINDOW = 512
LOGIT = math.log2(math.e) * HEAD_SIZE ** -0.5
F32 = jnp.float32
BF16 = jnp.bfloat16
TOKENS = 1024
CHIPS = 16
ROWS = 64
LT = 256
SPAN = LT + WINDOW


def scores(q, k):
    return lax.dot_general(q, k, (((1,), (1,)), ((), ())), preferred_element_type=F32)


def mix(p, v):
    return jnp.dot(p.astype(BF16), v, preferred_element_type=F32)


def fold(q, k, v, state, allowed=None):
    top, total, acc = state
    s = scores(q, k)
    if allowed is not None:
        s = jnp.where(allowed, s, NEG)
    new_top = jnp.maximum(top, jnp.max(s, axis=-1, keepdims=True))
    p = jnp.exp2((s - new_top) * LOGIT)
    shrink = jnp.exp2((top - new_top) * LOGIT)
    total = shrink * total + jnp.sum(p, axis=-1, keepdims=True)
    acc = shrink * acc + mix(p, v)
    return new_top, total, acc


def iota(shape, dim):
    return lax.broadcasted_iota(jnp.int32, shape, dim)


SHIFTS = (2, 1, 3, 0)
PART = 32


def kernel(
    q_hbm, k_hbm, v_hbm, w_hbm, out_ref,
    q, kv, stage_q, stage_kv, rq, rkv, own_sum, summ, near, far, ret_out, ret, att_out, att, wbuf,
    in_sem, halo_sem, q_send, q_recv, kv_send, kv_recv, pair_send, pair_recv,
    sz_send, sz_recv, sx_send, sx_recv, sp_send, sp_recv,
    wz_send, wz_recv, wy_send, wy_recv, wx_send, wx_recv, wp_send, wp_recv,
    r_send, r_recv, own_sem, a_send, a_recv,
):
    c = lax.axis_index("ctx")
    h = lax.axis_index("head")
    core, x, zh = c % 2, (c // 2) % 4, c // 8
    zl, y = h % 2, h // 2
    chip = zh * 4 + x
    sib = (c + 1 - 2 * core, h)
    sends = []

    def remote(src, dst, ssem, rsem, dev):
        return pltpu.make_async_remote_copy(
            src_ref=src, dst_ref=dst, send_sem=ssem, recv_sem=rsem,
            device_id=dev, device_id_type=MESH,
        )

    def go(src, dst, ssem, rsem, dev):
        copy = remote(src, dst, ssem, rsem, dev)
        copy.start()
        sends.append(copy)

    def got(ref, sem):
        remote(ref, ref, sem, sem, sib).wait_recv()

    def chip_at(dz, dx):
        return ((zh + dz) % 4) * 4 + (x + dx) % 4

    def source(dz, dx):
        return ((zh - dz + 4) % 4) * 4 + (x - dx + 4) % 4

    def block(i):
        return (y // 2 + SHIFTS[i]) % 4

    offs = [(dz, dx) for dz in (2, 1, 3, 0) for dx in (2, 1, 3, 0) if dz or dx]
    quads = [(a, b) for a in range(2) for b in range(2)]

    loads = [
        pltpu.make_async_copy(q_hbm, q, in_sem.at[0]),
        pltpu.make_async_copy(k_hbm, kv.at[0, pl.ds(WINDOW, TOKENS)], in_sem.at[1]),
        pltpu.make_async_copy(v_hbm, kv.at[1, pl.ds(WINDOW, TOKENS)], in_sem.at[2]),
        pltpu.make_async_copy(w_hbm, wbuf.at[h], in_sem.at[3]),
    ]
    for load in loads:
        load.start()

    barrier = pltpu.get_barrier_semaphore()

    def greet(dev):
        pl.semaphore_signal(barrier, inc=1, device_id=dev, device_id_type=MESH)

    zfar = (((zh + 2 * zl - 1 + 4) % 4) * 8 + x * 2 + core, 2 * y + 1 - zl)
    zpeer = (c, 2 * y + 1 - zl)
    for dz, dx in offs:
        greet((chip_at(dz, dx) * 2 + core, h))
    for dy in (4, 3, 5, 2, 6, 1, 7, 0):
        for dz in (1, 0):
            if dy or dz:
                greet((c, ((y + dy) % 8) * 2 + (zl + dz) % 2))
    greet(((c + 2 * core - 1) % 32, h))
    greet(zfar)
    greet(sib)

    for load in loads[:3]:
        load.wait()

    ri, ci = iota((256, 256), 0), iota((256, 256), 1)
    swap = jnp.where(((ri >> 4) == (ci & 15)) & ((ri & 15) == (ci >> 4)), 1.0, 0.0).astype(BF16)
    for n in range(2):
        parts = [
            kv[n, pl.ds(WINDOW + 128 * g + 112, 16), :].astype(F32)[8:] for g in range(8)
        ]
        own_sum[n] = jnp.concatenate(parts, axis=0).astype(BF16)
        for b in range(4):
            rows = kv[n, pl.ds(WINDOW + 256 * b, 256), :]
            moved = jnp.dot(swap, rows, preferred_element_type=F32).astype(BF16)
            stage_kv[:, n, pl.ds(16 * b, 16), :] = moved.reshape(CHIPS, 16, HEAD_SIZE)
    for i in range(4):
        rows = q[pl.ds(pl.multiple_of(256 * block(i), 256), 256), :]
        moved = jnp.dot(swap, rows, preferred_element_type=F32).astype(BF16)
        stage_q[i] = moved.reshape(CHIPS, 16, HEAD_SIZE)

    rr, cc = iota((LT, SPAN), 0), iota((LT, SPAN), 1)

    def local_tile(i, bias):
        rows = pl.ds(pl.multiple_of(i * LT, LT), LT)
        window = pl.ds(pl.multiple_of(i * LT, LT), SPAN)
        s = scores(q[rows, :], kv[0, window, :])
        allowed = (cc > rr) & (cc <= rr + WINDOW)
        if bias:
            start = jnp.where(c == 0, WINDOW - i * LT, 0)
            allowed = allowed & (cc >= start)
        s = jnp.where(allowed, s, NEG)
        top = jnp.max(s, axis=-1, keepdims=True)
        p = jnp.exp2((s - top) * LOGIT)
        total = jnp.sum(p, axis=-1, keepdims=True)
        near[rows, :] = mix(p, kv[1, window, :]) / total

    half = WINDOW // LT

    @pl.loop(half, TOKENS // LT)
    def _(i):
        local_tile(i, False)

    pl.semaphore_wait(barrier, 33)

    STEP = (1, 7)
    side = x % 2
    xnext = (zh * 8 + (x + 1 - 2 * side) * 2 + core, h)

    def w_piece(yy, kind, k, p):
        zz = zl if kind == 0 else 1 - zl
        start = pl.multiple_of(64 * k + PART * ((side + p) % 2), PART)
        return wbuf.at[2 * (yy % 8) + zz, pl.ds(start, PART), :]

    orders = [
        [
            (kind, s, p)
            for kind in range(2)
            for s in range(4 - (kind != d))
            for p in range(2 if s < 2 else 1)
        ]
        for d in range(2)
    ]
    place = [{key: n for n, key in enumerate(orders[d])} for d in range(2)]
    distant = [(d, key) for d in range(2) for key in orders[d] if key[1] >= 2]
    w_count = len(orders[0])

    def w_send(d, key):
        kind, s, p = key
        ref = w_piece(y + (8 - STEP[d]) * s, kind, core, p)
        n = place[d][key]
        go(ref, ref, wy_send.at[d, n], wy_recv.at[d, n], (c, 2 * ((y + STEP[d]) % 8) + zl))

    def w_pair(ref, n):
        go(ref, ref, wp_send.at[n], wp_recv.at[n], sib)

    def w_got(d, key, k, other=0):
        kind, s, p = key
        return w_piece(y + (8 - STEP[d]) * (s + 1), kind, k, p + other)

    def w_relay(*numbers):
        for n in numbers:
            for d in range(2):
                key = orders[d][n]
                kind, s, p = key
                ref = w_got(d, key, core)
                got(ref, wy_recv.at[d, n])
                if (kind, s + 1, p) in place[d]:
                    w_send(d, (kind, s + 1, p))
                if s >= 2:
                    m = distant.index((d, key))
                    go(ref, ref, wx_send.at[m], wx_recv.at[m], xnext)
                w_pair(ref, 2 + w_count * d + n)

    def w_cross(*numbers):
        for m in numbers:
            ref = w_got(*distant[m], core, 1)
            got(ref, wx_recv.at[m])
            w_pair(ref, 2 + 2 * w_count + m)

    def w_swap():
        for p, dev in enumerate((zpeer, zfar)):
            start = pl.multiple_of(64 * core + PART * p, PART)
            ref = wbuf.at[h, pl.ds(start, PART), :]
            go(ref, ref, wz_send.at[p], wz_recv.at[p], dev)

    def w_other_part(p, k):
        return wbuf.at[2 * y + 1 - zl, pl.ds(pl.multiple_of(64 * k + PART * p, PART), PART), :]

    def w_other():
        for p in range(2):
            ref = w_other_part(p, core)
            got(ref, wz_recv.at[p])
            w_pair(ref, p)
        for p in range(2):
            w_send(0, (1, 0, p))
            w_send(1, (1, 0, p))

    def w_finish():
        for p in range(2):
            got(w_other_part(p, 1 - core), wp_recv.at[p])
        for d in range(2):
            for n, key in enumerate(orders[d]):
                got(w_got(d, key, 1 - core), wp_recv.at[2 + w_count * d + n])
        for m, (d, key) in enumerate(distant):
            got(w_got(d, key, 1 - core, 1), wp_recv.at[2 + 2 * w_count + m])

    for n, dz in enumerate((2, 1, 3)):
        dev = (((zh + dz) % 4) * 8 + x * 2 + core, h)
        go(own_sum, summ.at[:, zh, x, core], sz_send.at[n], sz_recv.at[n], dev)
    loads[3].wait()
    for p in range(2):
        w_send(0, (0, 0, p))
        w_send(1, (0, 0, p))
    for n, (dz, dx) in enumerate(offs):
        to = chip_at(dz, dx)
        go(stage_kv.at[to], rkv.at[:, chip, core], kv_send.at[n], kv_recv.at[n], (to * 2 + core, h))
    w_swap()
    for i in range(4):
        for n, (dz, dx) in enumerate(offs):
            to = chip_at(dz, dx)
            go(stage_q.at[i, to], rq.at[i, chip], q_send.at[i, n], q_recv.at[i, n], (to * 2 + core, h))
    halo_to = kv.at[:, pl.ds(0, WINDOW)]
    go(kv.at[:, pl.ds(TOKENS, WINDOW)], halo_to, halo_sem.at[0], halo_sem.at[1], ((c + 1) % 32, h))
    own = [
        pltpu.make_async_copy(stage_kv.at[chip], rkv.at[:, chip, core], in_sem.at[4]),
        pltpu.make_async_copy(stage_q.at[:, chip], rq.at[:, chip], in_sem.at[5]),
        pltpu.make_async_copy(own_sum, summ.at[:, zh, x, core], in_sem.at[6]),
    ]
    for copy in own:
        copy.start()
    go(stage_kv.at[chip], rkv.at[:, chip, core], pair_send.at[15], pair_recv.at[15], sib)

    def take_pairs(numbers):
        for n in numbers:
            ref = rkv.at[:, source(*offs[n]), core]
            got(ref, kv_recv.at[n])
            go(ref, ref, pair_send.at[n], pair_recv.at[n], sib)

    qrow = iota((256, 512), 0)
    kcol = iota((256, 512), 1)

    def summary_tile(i):
        b = block(i)
        rows = pl.ds(pl.multiple_of(b * 256, 256), 256)
        qs = q[rows, :]
        own_rows = pl.ds(pl.multiple_of(WINDOW + b * 256, 256), 256)
        ks = kv[0, own_rows, :].astype(F32)
        vs = kv[1, own_rows, :].astype(F32)
        self_score = jnp.sum(qs.astype(F32) * ks, axis=-1, keepdims=True)
        apart = (iota((256, 1), 0) & 127) < 120
        state = (
            jnp.where(apart, self_score, NEG),
            jnp.where(apart, 1.0, 0.0),
            jnp.where(apart, vs, 0.0),
        )

        def step(t, state):
            return fold(
                qs, summ[0, t].reshape(512, HEAD_SIZE), summ[1, t].reshape(512, HEAD_SIZE), state
            )

        state = lax.fori_loop(0, zh, step, state)
        at = qrow + (b * 256 + (2 * x + core) * TOKENS)
        key_at = (kcol >> 3) * 128 + 120 + (kcol & 7)
        state = fold(
            qs, summ[0, zh].reshape(512, HEAD_SIZE), summ[1, zh].reshape(512, HEAD_SIZE),
            state, key_at <= at,
        )
        far[rows, :] = state[2] / state[1]

    def summary_spread():
        own[2].wait()
        for n, dz in enumerate((2, 1, 3)):
            got(summ.at[:, (zh - dz + 4) % 4, x, core], sz_recv.at[n])
        ref = summ.at[:, :, x, core]
        for n, dx in enumerate((2, 1, 3)):
            dev = (zh * 8 + ((x + dx) % 4) * 2 + core, h)
            go(ref, ref, sx_send.at[n], sx_recv.at[n], dev)
        go(ref, ref, sp_send.at[3], sp_recv.at[3], sib)

    def summary_pair():
        for n, dx in enumerate((2, 1, 3)):
            ref = summ.at[:, :, (x - dx + 4) % 4, core]
            got(ref, sx_recv.at[n])
            go(ref, ref, sp_send.at[n], sp_recv.at[n], sib)

    def summary_ready():
        for n, dx in enumerate((2, 1, 3, 0)):
            got(summ.at[:, :, (x - dx + 4) % 4, 1 - core], sp_recv.at[n])

    def strided_ready():
        own[0].wait()
        own[1].wait()
        for n in range(15):
            got(rkv.at[:, source(*offs[n]), 1 - core], pair_recv.at[n])
        got(rkv.at[:, chip, 1 - core], pair_recv.at[15])

    drow, dcol = iota((64, 512), 0), iota((64, 512), 1)

    def stride_block(i):
        for n in range(15):
            got(rq.at[i, source(*offs[n])], q_recv.at[i, n])
        qs = rq[i].reshape(256, HEAD_SIZE)
        allowed = dcol <= (drow >> 4) * 128 + (drow & 15) + (core * 64 + block(i) * 16)
        state = None
        for t in range(4):
            ks = rkv[0, pl.ds(t * 4, 4)].reshape(512, HEAD_SIZE)
            vs = rkv[1, pl.ds(t * 4, 4)].reshape(512, HEAD_SIZE)
            s = scores(qs[64 * t :], ks)
            first = jnp.where(allowed, s[:64], NEG)
            s = first if t == 3 else jnp.concatenate([first, s[64:]], axis=0)
            top = jnp.max(s, axis=-1, keepdims=True)
            if t:
                top = jnp.maximum(top, state[0])
            p = jnp.exp2((s - top) * LOGIT)
            total = jnp.sum(p, axis=-1, keepdims=True)
            acc = mix(p, vs)
            if t:
                shrink = jnp.exp2((state[0] - top) * LOGIT)
                total = total + shrink * state[1]
                acc = acc + shrink * state[2]
            done = (acc[:64] / total[:64]).astype(BF16)
            ret_out[i, pl.ds(4 * t, 4)] = done.reshape(4, 16, HEAD_SIZE)
            if t < 3:
                state = (top[64:], total[64:], acc[64:])
        for n, (dz, dx) in enumerate(offs):
            to = chip_at(dz, dx)
            go(ret_out.at[i, to], ret.at[i, chip], r_send.at[i, n], r_recv.at[i, n], (to * 2 + core, h))
        pltpu.make_async_copy(ret_out.at[i, chip], ret.at[i, chip], own_sem.at[i]).start()

    def join_block(i):
        pltpu.make_async_copy(ret_out.at[i, chip], ret.at[i, chip], own_sem.at[i]).wait()
        for n in range(15):
            got(ret.at[i, source(*offs[n])], r_recv.at[i, n])
        rows = pl.ds(pl.multiple_of(block(i) * 256, 256), 256)
        strided = jnp.dot(swap, ret[i].reshape(256, HEAD_SIZE), preferred_element_type=F32)
        att_out[i] = (near[rows, :] + far[rows, :] + strided).astype(BF16)
        for m, (dy, dz) in enumerate(quads):
            yy, zz = (y + dy) % 2, (zl + dz) % 2
            part = att_out.at[i, pl.ds(pl.multiple_of(64 * (2 * yy + zz), 64), 64)]
            if SHIFTS[i] or dy or dz:
                dev = (c, 4 * block(i) + 2 * yy + zz)
                go(part, att.at[h], a_send.at[i, m], a_recv.at[i, m], dev)
            else:
                pltpu.make_async_copy(part, att.at[h], own_sem.at[4]).start()

    def attended_ready():
        for i in range(4):
            for m, (dy, dz) in enumerate(quads):
                src = 4 * ((y // 2 - SHIFTS[i] + 4) % 4) + 2 * ((y + dy) % 2) + (zl + dz) % 2
                if SHIFTS[i] or dy or dz:
                    got(att.at[src], a_recv.at[i, m])
                else:
                    pltpu.make_async_copy(att.at[src], att.at[src], own_sem.at[4]).wait()

    w_relay(0)
    summary_spread()
    w_relay(1, 2)
    take_pairs(range(0, 5))
    w_relay(3)
    summary_pair()
    take_pairs(range(5, 15))
    w_relay(4)
    summary_ready()
    summary_tile(0)
    w_other()
    summary_tile(1)
    w_relay(5)
    strided_ready()
    stride_block(0)
    stride_block(1)
    w_relay(6)
    stride_block(2)
    stride_block(3)
    w_relay(7)
    got(halo_to, halo_sem.at[1])

    @pl.loop(0, half)
    def _(i):
        local_tile(i, True)

    join_block(0)
    w_relay(8)
    summary_tile(2)
    join_block(1)
    summary_tile(3)
    w_relay(9)
    join_block(2)
    join_block(3)
    w_cross(0, 1, 3)
    w_relay(10)
    w_cross(2, 4, 5)
    attended_ready()
    w_finish()

    rows = jnp.concatenate([att[i] for i in range(16)], axis=-1)

    @pl.loop(0, 4)
    def _(n):
        cols = pl.ds(pl.multiple_of(n * 512, 512), 512)
        weights = wbuf[:, :, cols].reshape(2048, 512)
        out_ref[:, cols] = jnp.dot(rows, weights, preferred_element_type=F32).astype(BF16)

    for copy in sends:
        copy.wait_send()


def body(queries, keys, values, out_weight):
    dma = pltpu.SemaphoreType.DMA
    wide = (CHIPS, 16, HEAD_SIZE)
    return pl.pallas_call(
        kernel,
        out_shape=jax.ShapeDtypeStruct((64, 2048), BF16),
        in_specs=[pl.BlockSpec(memory_space=pl.ANY)] * 4,
        out_specs=pl.BlockSpec(memory_space=pltpu.VMEM),
        scratch_shapes=[
            pltpu.VMEM((TOKENS, HEAD_SIZE), BF16),
            pltpu.VMEM((2, WINDOW + TOKENS, HEAD_SIZE), BF16),
            pltpu.VMEM((4, *wide), BF16),
            pltpu.VMEM((CHIPS, 2, ROWS, HEAD_SIZE), BF16),
            pltpu.VMEM((4, *wide), BF16),
            pltpu.VMEM((2, CHIPS, 2, ROWS, HEAD_SIZE), BF16),
            pltpu.VMEM((2, ROWS, HEAD_SIZE), BF16),
            pltpu.VMEM((2, 4, 4, 2, ROWS, HEAD_SIZE), BF16),
            pltpu.VMEM((TOKENS, HEAD_SIZE), F32),
            pltpu.VMEM((TOKENS, HEAD_SIZE), F32),
            pltpu.VMEM((4, *wide), BF16),
            pltpu.VMEM((4, *wide), BF16),
            pltpu.VMEM((4, 256, HEAD_SIZE), BF16),
            pltpu.VMEM((16, 64, HEAD_SIZE), BF16),
            pltpu.VMEM((16, HEAD_SIZE, 2048), BF16),
            dma((7,)), dma((2,)), dma((4, 15)), dma((4, 15)), dma((15,)), dma((15,)),
            dma((16,)), dma((16,)),
            dma((3,)), dma((3,)), dma((3,)), dma((3,)), dma((4,)), dma((4,)),
            dma((2,)), dma((2,)), dma((2, 11)), dma((2, 11)), dma((6,)), dma((6,)),
            dma((30,)), dma((30,)),
            dma((4, 15)), dma((4, 15)), dma((5,)), dma((4, 4)), dma((4, 4)),
        ],
        compiler_params=pltpu.CompilerParams(collective_id=0, has_side_effects=True),
    )(queries, keys, values, out_weight)


def solution(mesh):
    placed = (P("ctx", "head"), P("ctx", "head"), P("ctx", "head"), P("head", None))
    return jax.shard_map(
        body, mesh=mesh, in_specs=placed, out_specs=P(("ctx", "head"), None), check_vma=False
    )
```

time: 92.1 us -> 77.1 us (0.84)
  Pallas kernels: 90.3 us -> 75.2 us
    pallas_call x1, Pallas kernels: 90.3 us -> 75.2 us  [body(): pl.pallas_call(kernel, out_shape=jax.ShapeDtypeStruct((64, 2048), BF16),...]
where the time goes in v2:
time: 77.1 us; the launch traced here: 76.9 us
  Pallas kernels  75.2 us (98%)
  local copies, waits for them, and re-layouts  1.67 us (2%)
    pallas_call x1, Pallas kernels, body(): pl.pallas_call(kernel, out_shape=jax.ShapeDtypeStruct((64, 2048), BF16),...  75.2 us
    unnamed x1, local copies, waits for them, and re-layouts  1.67 us

profile of v2, /device:TPU:3, one launch (start us, length us, event | category | flops | bytes accessed | tf_op | source)
XLA Modules:
  0.0 76.9 jit_solution(13175712121875145015)
XLA Ops:
  0.0 75.2 %shard_map.46 = bf16[64,2048]{1,0:T(8,128)(2,1)} custom-call(bf16[1024,128]{1,0:T(8,128)(2,1)} %q_hbm.1, bf16[1024,128]{1,0:T(8,128)(2,1)} %k_hbm.1, bf16[1024,128]{1,0:T(8,128)(2,1)} %v_hbm.1, bf16[128,2048]{1,0:T(8,128)(2,1)} %w_hbm.1), custom_call_target="tpu_custom_call" | custom-call | tf_op jit(solution)/shard_map/pallas_call | solution.py:451
  75.2 1.7 %copy.6 = bf16[64,2048]{1,0:T(8,128)(2,1)} copy(bf16[64,2048]{1,0:T(8,128)(2,1)} %shard_map.46) | data formatting | bytes 524288

commit v3 on v2

--- a/solution.py
+++ b/solution.py
@@ -174,9 +174,10 @@
     orders = [
         [
             (kind, s, p)
+            for s in range(4)
             for kind in range(2)
-            for s in range(4 - (kind != d))
             for p in range(2 if s < 2 else 1)
+            if s < 3 or kind == d
         ]
         for d in range(2)
     ]
@@ -244,17 +245,17 @@
         for m, (d, key) in enumerate(distant):
             got(w_got(d, key, 1 - core, 1), wp_recv.at[2 + 2 * w_count + m])
 
+    loads[3].wait()
+    w_swap()
+    for p in range(2):
+        w_send(0, (0, 0, p))
+        w_send(1, (0, 0, p))
     for n, dz in enumerate((2, 1, 3)):
         dev = (((zh + dz) % 4) * 8 + x * 2 + core, h)
         go(own_sum, summ.at[:, zh, x, core], sz_send.at[n], sz_recv.at[n], dev)
-    loads[3].wait()
-    for p in range(2):
-        w_send(0, (0, 0, p))
-        w_send(1, (0, 0, p))
     for n, (dz, dx) in enumerate(offs):
         to = chip_at(dz, dx)
         go(stage_kv.at[to], rkv.at[:, chip, core], kv_send.at[n], kv_recv.at[n], (to * 2 + core, h))
-    w_swap()
     for i in range(4):
         for n, (dz, dx) in enumerate(offs):
             to = chip_at(dz, dx)
@@ -393,19 +394,21 @@
                 else:
                     pltpu.make_async_copy(att.at[src], att.at[src], own_sem.at[4]).wait()
 
+    w_other()
     w_relay(0)
     summary_spread()
     w_relay(1, 2)
-    take_pairs(range(0, 5))
+    summary_pair()
     w_relay(3)
-    summary_pair()
-    take_pairs(range(5, 15))
-    w_relay(4)
+    take_pairs(range(0, 4))
     summary_ready()
     summary_tile(0)
-    w_other()
+    w_relay(4)
+    take_pairs(range(4, 10))
     summary_tile(1)
     w_relay(5)
+    take_pairs(range(10, 15))
+    summary_tile(2)
     strided_ready()
     stride_block(0)
     stride_block(1)
@@ -413,6 +416,7 @@
     stride_block(2)
     stride_block(3)
     w_relay(7)
+    summary_tile(3)
     got(halo_to, halo_sem.at[1])
 
     @pl.loop(0, half)
@@ -420,16 +424,14 @@
         local_tile(i, True)
 
     join_block(0)
+    join_block(1)
     w_relay(8)
-    summary_tile(2)
-    join_block(1)
-    summary_tile(3)
-    w_relay(9)
     join_block(2)
     join_block(3)
-    w_cross(0, 1, 3)
+    w_relay(9)
+    w_cross(0, 3)
     w_relay(10)
-    w_cross(2, 4, 5)
+    w_cross(1, 4, 2, 5)
     attended_ready()
     w_finish()
 

time: 77.1 us -> 88.1 us (1.14)
  the two profiles are of different devices: /device:TPU:3 before, /device:TPU:97 now
where the time goes in v3:
time: 88.1 us; the launch traced here: 87.9 us
  Pallas kernels  86.2 us (98%)
  local copies, waits for them, and re-layouts  1.67 us (2%)
    pallas_call x1, Pallas kernels, body(): pl.pallas_call(kernel, out_shape=jax.ShapeDtypeStruct((64, 2048), BF16),...  86.2 us

profile of v3, /device:TPU:97, one launch (start us, length us, event | category | flops | bytes accessed | tf_op | source)
XLA Modules:
  0.0 87.9 jit_solution(5191047281738687349)
XLA Ops:
  0.0 86.2 %shard_map.46 = bf16[64,2048]{1,0:T(8,128)(2,1)} custom-call(bf16[1024,128]{1,0:T(8,128)(2,1)} %q_hbm.1, bf16[1024,128]{1,0:T(8,128)(2,1)} %k_hbm.1, bf16[1024,128]{1,0:T(8,128)(2,1)} %v_hbm.1, bf16[128,2048]{1,0:T(8,128)(2,1)} %w_hbm.1), custom_call_target="tpu_custom_call" | custom-call | tf_op jit(solution)/shard_map/pallas_call | solution.py:453
  86.2 1.7 %copy.6 = bf16[64,2048]{1,0:T(8,128)(2,1)} copy(bf16[64,2048]{1,0:T(8,128)(2,1)} %shard_map.46) | data formatting | bytes 524288

commit v4 on v3

--- a/solution.py
+++ b/solution.py
@@ -47,7 +47,7 @@
     return lax.broadcasted_iota(jnp.int32, shape, dim)
 
 
-SHIFTS = (2, 1, 3, 0)
+SHIFTS = (1, 0)
 PART = 32
 
 
@@ -87,16 +87,19 @@
     def source(dz, dx):
         return ((zh - dz + 4) % 4) * 4 + (x - dx + 4) % 4
 
+    def half_block(i):
+        return (y // 4 + SHIFTS[i]) % 2
+
     def block(i):
-        return (y // 2 + SHIFTS[i]) % 4
+        return 2 * half_block(i // 2) + i % 2
 
     offs = [(dz, dx) for dz in (2, 1, 3, 0) for dx in (2, 1, 3, 0) if dz or dx]
-    quads = [(a, b) for a in range(2) for b in range(2)]
+    octs = [(a, b) for a in (2, 1, 3, 0) for b in (1, 0)]
 
     loads = [
-        pltpu.make_async_copy(q_hbm, q, in_sem.at[0]),
         pltpu.make_async_copy(k_hbm, kv.at[0, pl.ds(WINDOW, TOKENS)], in_sem.at[1]),
         pltpu.make_async_copy(v_hbm, kv.at[1, pl.ds(WINDOW, TOKENS)], in_sem.at[2]),
+        pltpu.make_async_copy(q_hbm, q, in_sem.at[0]),
         pltpu.make_async_copy(w_hbm, wbuf.at[h], in_sem.at[3]),
     ]
     for load in loads:
@@ -119,7 +122,7 @@
     greet(zfar)
     greet(sib)
 
-    for load in loads[:3]:
+    for load in loads[:2]:
         load.wait()
 
     ri, ci = iota((256, 256), 0), iota((256, 256), 1)
@@ -133,11 +136,6 @@
             rows = kv[n, pl.ds(WINDOW + 256 * b, 256), :]
             moved = jnp.dot(swap, rows, preferred_element_type=F32).astype(BF16)
             stage_kv[:, n, pl.ds(16 * b, 16), :] = moved.reshape(CHIPS, 16, HEAD_SIZE)
-    for i in range(4):
-        rows = q[pl.ds(pl.multiple_of(256 * block(i), 256), 256), :]
-        moved = jnp.dot(swap, rows, preferred_element_type=F32).astype(BF16)
-        stage_q[i] = moved.reshape(CHIPS, 16, HEAD_SIZE)
-
     rr, cc = iota((LT, SPAN), 0), iota((LT, SPAN), 1)
 
     def local_tile(i, bias):
@@ -156,15 +154,13 @@
 
     half = WINDOW // LT
 
-    @pl.loop(half, TOKENS // LT)
-    def _(i):
-        local_tile(i, False)
-
     pl.semaphore_wait(barrier, 33)
 
     STEP = (1, 7)
     side = x % 2
     xnext = (zh * 8 + (x + 1 - 2 * side) * 2 + core, h)
+
+    xother = (zh * 8 + ((x + 2 * side + 3) % 4) * 2 + core, h)
 
     def w_piece(yy, kind, k, p):
         zz = zl if kind == 0 else 1 - zl
@@ -176,13 +172,13 @@
             (kind, s, p)
             for s in range(4)
             for kind in range(2)
-            for p in range(2 if s < 2 else 1)
+            for p in range(1 if s else 2)
             if s < 3 or kind == d
         ]
         for d in range(2)
     ]
     place = [{key: n for n, key in enumerate(orders[d])} for d in range(2)]
-    distant = [(d, key) for d in range(2) for key in orders[d] if key[1] >= 2]
+    distant = [(d, key) for d in range(2) for key in orders[d] if key[1]]
     w_count = len(orders[0])
 
     def w_send(d, key):
@@ -207,9 +203,9 @@
                 got(ref, wy_recv.at[d, n])
                 if (kind, s + 1, p) in place[d]:
                     w_send(d, (kind, s + 1, p))
-                if s >= 2:
+                if s:
                     m = distant.index((d, key))
-                    go(ref, ref, wx_send.at[m], wx_recv.at[m], xnext)
+                    go(ref, ref, wx_send.at[m], wx_recv.at[m], xnext if s > 1 else xother)
                 w_pair(ref, 2 + w_count * d + n)
 
     def w_cross(*numbers):
@@ -245,31 +241,38 @@
         for m, (d, key) in enumerate(distant):
             got(w_got(d, key, 1 - core, 1), wp_recv.at[2 + 2 * w_count + m])
 
+    for n, dz in enumerate((2, 1, 3)):
+        dev = (((zh + dz) % 4) * 8 + x * 2 + core, h)
+        go(own_sum, summ.at[:, zh, x, core], sz_send.at[n], sz_recv.at[n], dev)
     loads[3].wait()
     w_swap()
     for p in range(2):
         w_send(0, (0, 0, p))
         w_send(1, (0, 0, p))
-    for n, dz in enumerate((2, 1, 3)):
-        dev = (((zh + dz) % 4) * 8 + x * 2 + core, h)
-        go(own_sum, summ.at[:, zh, x, core], sz_send.at[n], sz_recv.at[n], dev)
+    loads[2].wait()
+    for b in range(4):
+        moved = jnp.dot(swap, q[pl.ds(256 * b, 256), :], preferred_element_type=F32).astype(BF16)
+        stage_q[:, pl.ds(16 * b, 16), :] = moved.reshape(CHIPS, 16, HEAD_SIZE)
     for n, (dz, dx) in enumerate(offs):
         to = chip_at(dz, dx)
         go(stage_kv.at[to], rkv.at[:, chip, core], kv_send.at[n], kv_recv.at[n], (to * 2 + core, h))
-    for i in range(4):
-        for n, (dz, dx) in enumerate(offs):
-            to = chip_at(dz, dx)
-            go(stage_q.at[i, to], rq.at[i, chip], q_send.at[i, n], q_recv.at[i, n], (to * 2 + core, h))
+    for n, (dz, dx) in enumerate(offs):
+        to = chip_at(dz, dx)
+        go(stage_q.at[to], rq.at[chip], q_send.at[n], q_recv.at[n], (to * 2 + core, h))
     halo_to = kv.at[:, pl.ds(0, WINDOW)]
     go(kv.at[:, pl.ds(TOKENS, WINDOW)], halo_to, halo_sem.at[0], halo_sem.at[1], ((c + 1) % 32, h))
     own = [
         pltpu.make_async_copy(stage_kv.at[chip], rkv.at[:, chip, core], in_sem.at[4]),
-        pltpu.make_async_copy(stage_q.at[:, chip], rq.at[:, chip], in_sem.at[5]),
+        pltpu.make_async_copy(stage_q.at[chip], rq.at[chip], in_sem.at[5]),
         pltpu.make_async_copy(own_sum, summ.at[:, zh, x, core], in_sem.at[6]),
     ]
     for copy in own:
         copy.start()
     go(stage_kv.at[chip], rkv.at[:, chip, core], pair_send.at[15], pair_recv.at[15], sib)
+
+    @pl.loop(half, TOKENS // LT)
+    def _(i):
+        local_tile(i, False)
 
     def take_pairs(numbers):
         for n in numbers:
@@ -335,14 +338,15 @@
         for n in range(15):
             got(rkv.at[:, source(*offs[n]), 1 - core], pair_recv.at[n])
         got(rkv.at[:, chip, 1 - core], pair_recv.at[15])
+        for n in range(15):
+            got(rq.at[source(*offs[n])], q_recv.at[n])
 
     drow, dcol = iota((64, 512), 0), iota((64, 512), 1)
 
-    def stride_block(i):
-        for n in range(15):
-            got(rq.at[i, source(*offs[n])], q_recv.at[i, n])
-        qs = rq[i].reshape(256, HEAD_SIZE)
-        allowed = dcol <= (drow >> 4) * 128 + (drow & 15) + (core * 64 + block(i) * 16)
+    def strided_rows(i, u):
+        b = 2 * half_block(i) + u
+        qs = rq[:, pl.ds(pl.multiple_of(16 * b, 16), 16), :].reshape(256, HEAD_SIZE)
+        allowed = dcol <= (drow >> 4) * 128 + (drow & 15) + (core * 64 + b * 16)
         state = None
         for t in range(4):
             ks = rkv[0, pl.ds(t * 4, 4)].reshape(512, HEAD_SIZE)
@@ -361,9 +365,13 @@
                 total = total + shrink * state[1]
                 acc = acc + shrink * state[2]
             done = (acc[:64] / total[:64]).astype(BF16)
-            ret_out[i, pl.ds(4 * t, 4)] = done.reshape(4, 16, HEAD_SIZE)
+            ret_out[i, pl.ds(4 * t, 4), pl.ds(16 * u, 16)] = done.reshape(4, 16, HEAD_SIZE)
             if t < 3:
                 state = (top[64:], total[64:], acc[64:])
+
+    def stride_block(i):
+        for u in range(2):
+            strided_rows(i, u)
         for n, (dz, dx) in enumerate(offs):
             to = chip_at(dz, dx)
             go(ret_out.at[i, to], ret.at[i, chip], r_send.at[i, n], r_recv.at[i, n], (to * 2 + core, h))
@@ -373,26 +381,28 @@
         pltpu.make_async_copy(ret_out.at[i, chip], ret.at[i, chip], own_sem.at[i]).wait()
         for n in range(15):
             got(ret.at[i, source(*offs[n])], r_recv.at[i, n])
-        rows = pl.ds(pl.multiple_of(block(i) * 256, 256), 256)
-        strided = jnp.dot(swap, ret[i].reshape(256, HEAD_SIZE), preferred_element_type=F32)
-        att_out[i] = (near[rows, :] + far[rows, :] + strided).astype(BF16)
-        for m, (dy, dz) in enumerate(quads):
-            yy, zz = (y + dy) % 2, (zl + dz) % 2
+        for u in range(2):
+            rows = pl.ds(pl.multiple_of((2 * half_block(i) + u) * 256, 256), 256)
+            part = ret[i, :, pl.ds(16 * u, 16), :].reshape(256, HEAD_SIZE)
+            strided = jnp.dot(swap, part, preferred_element_type=F32)
+            att_out[i, pl.ds(256 * u, 256), :] = (near[rows, :] + far[rows, :] + strided).astype(BF16)
+        for m, (dy, dz) in enumerate(octs):
+            yy, zz = (y + dy) % 4, (zl + dz) % 2
             part = att_out.at[i, pl.ds(pl.multiple_of(64 * (2 * yy + zz), 64), 64)]
             if SHIFTS[i] or dy or dz:
-                dev = (c, 4 * block(i) + 2 * yy + zz)
+                dev = (c, 8 * half_block(i) + 2 * yy + zz)
                 go(part, att.at[h], a_send.at[i, m], a_recv.at[i, m], dev)
             else:
-                pltpu.make_async_copy(part, att.at[h], own_sem.at[4]).start()
+                pltpu.make_async_copy(part, att.at[h], own_sem.at[2]).start()
 
     def attended_ready():
-        for i in range(4):
-            for m, (dy, dz) in enumerate(quads):
-                src = 4 * ((y // 2 - SHIFTS[i] + 4) % 4) + 2 * ((y + dy) % 2) + (zl + dz) % 2
+        for i in range(2):
+            for m, (dy, dz) in enumerate(octs):
+                src = 8 * half_block(i) + 2 * ((y - dy + 4) % 4) + (zl + dz) % 2
                 if SHIFTS[i] or dy or dz:
                     got(att.at[src], a_recv.at[i, m])
                 else:
-                    pltpu.make_async_copy(att.at[src], att.at[src], own_sem.at[4]).wait()
+                    pltpu.make_async_copy(att.at[src], att.at[src], own_sem.at[2]).wait()
 
     w_other()
     w_relay(0)
@@ -400,22 +410,20 @@
     w_relay(1, 2)
     summary_pair()
     w_relay(3)
-    take_pairs(range(0, 4))
+    take_pairs(range(0, 8))
+    w_relay(4)
+    take_pairs(range(8, 15))
+    w_relay(5)
+    strided_ready()
+    stride_block(0)
+    w_relay(6)
+    stride_block(1)
+    w_relay(7)
     summary_ready()
     summary_tile(0)
-    w_relay(4)
-    take_pairs(range(4, 10))
     summary_tile(1)
-    w_relay(5)
-    take_pairs(range(10, 15))
+    w_relay(8)
     summary_tile(2)
-    strided_ready()
-    stride_block(0)
-    stride_block(1)
-    w_relay(6)
-    stride_block(2)
-    stride_block(3)
-    w_relay(7)
     summary_tile(3)
     got(halo_to, halo_sem.at[1])
 
@@ -424,14 +432,9 @@
         local_tile(i, True)
 
     join_block(0)
+    w_cross(0, 5, 1, 6, 2, 7)
     join_block(1)
-    w_relay(8)
-    join_block(2)
-    join_block(3)
-    w_relay(9)
-    w_cross(0, 3)
-    w_relay(10)
-    w_cross(1, 4, 2, 5)
+    w_cross(3, 8, 4, 9)
     attended_ready()
     w_finish()
 
@@ -441,7 +444,7 @@
     def _(n):
         cols = pl.ds(pl.multiple_of(n * 512, 512), 512)
         weights = wbuf[:, :, cols].reshape(2048, 512)
-        out_ref[:, cols] = jnp.dot(rows, weights, preferred_element_type=F32).astype(BF16)
+        out_ref[:, cols] = jnp.dot(rows, weights, preferred_element_type=F32)
 
     for copy in sends:
         copy.wait_send()
@@ -449,37 +452,37 @@
 
 def body(queries, keys, values, out_weight):
     dma = pltpu.SemaphoreType.DMA
-    wide = (CHIPS, 16, HEAD_SIZE)
+    wide = (CHIPS, 32, HEAD_SIZE)
     return pl.pallas_call(
         kernel,
-        out_shape=jax.ShapeDtypeStruct((64, 2048), BF16),
+        out_shape=jax.ShapeDtypeStruct((64, 2048), F32),
         in_specs=[pl.BlockSpec(memory_space=pl.ANY)] * 4,
         out_specs=pl.BlockSpec(memory_space=pltpu.VMEM),
         scratch_shapes=[
             pltpu.VMEM((TOKENS, HEAD_SIZE), BF16),
             pltpu.VMEM((2, WINDOW + TOKENS, HEAD_SIZE), BF16),
-            pltpu.VMEM((4, *wide), BF16),
+            pltpu.VMEM((CHIPS, ROWS, HEAD_SIZE), BF16),
             pltpu.VMEM((CHIPS, 2, ROWS, HEAD_SIZE), BF16),
-            pltpu.VMEM((4, *wide), BF16),
+            pltpu.VMEM((CHIPS, ROWS, HEAD_SIZE), BF16),
             pltpu.VMEM((2, CHIPS, 2, ROWS, HEAD_SIZE), BF16),
             pltpu.VMEM((2, ROWS, HEAD_SIZE), BF16),
             pltpu.VMEM((2, 4, 4, 2, ROWS, HEAD_SIZE), BF16),
             pltpu.VMEM((TOKENS, HEAD_SIZE), F32),
             pltpu.VMEM((TOKENS, HEAD_SIZE), F32),
-            pltpu.VMEM((4, *wide), BF16),
-            pltpu.VMEM((4, *wide), BF16),
-            pltpu.VMEM((4, 256, HEAD_SIZE), BF16),
+            pltpu.VMEM((2, *wide), BF16),
+            pltpu.VMEM((2, *wide), BF16),
+            pltpu.VMEM((2, 512, HEAD_SIZE), BF16),
             pltpu.VMEM((16, 64, HEAD_SIZE), BF16),
             pltpu.VMEM((16, HEAD_SIZE, 2048), BF16),
-            dma((7,)), dma((2,)), dma((4, 15)), dma((4, 15)), dma((15,)), dma((15,)),
+            dma((7,)), dma((2,)), dma((15,)), dma((15,)), dma((15,)), dma((15,)),
             dma((16,)), dma((16,)),
             dma((3,)), dma((3,)), dma((3,)), dma((3,)), dma((4,)), dma((4,)),
-            dma((2,)), dma((2,)), dma((2, 11)), dma((2, 11)), dma((6,)), dma((6,)),
+            dma((2,)), dma((2,)), dma((2, 9)), dma((2, 9)), dma((10,)), dma((10,)),
             dma((30,)), dma((30,)),
-            dma((4, 15)), dma((4, 15)), dma((5,)), dma((4, 4)), dma((4, 4)),
+            dma((2, 15)), dma((2, 15)), dma((3,)), dma((2, 8)), dma((2, 8)),
         ],
         compiler_params=pltpu.CompilerParams(collective_id=0, has_side_effects=True),
-    )(queries, keys, values, out_weight)
+    )(queries, keys, values, out_weight).astype(BF16)
 
 
 def solution(mesh):

time: 88.1 us -> 74.3 us (0.84)
  the two profiles are of different devices: /device:TPU:97 before, /device:TPU:27 now
where the time goes in v4:
time: 74.3 us; the launch traced here: 74.1 us
  Pallas kernels  72.3 us (97%)
  other arithmetic  1.77 us (2%)
    pallas_call x1, Pallas kernels, body(): pl.pallas_call(kernel, out_shape=jax.ShapeDtypeStruct((64, 2048), F32), i...  72.3 us
    convert_element_type x1, other arithmetic, body(): return pl.pallas_call(kernel, out_shape=jax.ShapeDtypeStruct((64, 2048),...  1.77 us

profile of v4, /device:TPU:27, one launch (start us, length us, event | category | flops | bytes accessed | tf_op | source)
XLA Modules:
  0.0 74.1 jit_solution(16929811693924616648)
XLA Ops:
  0.0 72.3 %shard_map.46 = f32[64,2048]{1,0:T(8,128)} custom-call(bf16[1024,128]{1,0:T(8,128)(2,1)} %q_hbm.1, bf16[1024,128]{1,0:T(8,128)(2,1)} %k_hbm.1, bf16[1024,128]{1,0:T(8,128)(2,1)} %v_hbm.1, bf16[128,2048]{1,0:T(8,128)(2,1)} %w_hbm.1), custom_call_target="tpu_custom_call" | custom-call | tf_op jit(solution)/shard_map/pallas_call | solution.py:456
  72.4 1.8 %convert_element_type.3 = bf16[64,2048]{1,0:T(8,128)(2,1)} convert(f32[64,2048]{1,0:T(8,128)} %shard_map.46) | non-fusion elementwise | flops 131072 | bytes 786432 | tf_op jit(solution)/shard_map/convert_element_type | solution.py:485

commit v5 on v4

--- a/solution.py
+++ b/solution.py
@@ -423,8 +423,6 @@
     summary_tile(0)
     summary_tile(1)
     w_relay(8)
-    summary_tile(2)
-    summary_tile(3)
     got(halo_to, halo_sem.at[1])
 
     @pl.loop(0, half)
@@ -432,7 +430,10 @@
         local_tile(i, True)
 
     join_block(0)
-    w_cross(0, 5, 1, 6, 2, 7)
+    summary_tile(2)
+    w_cross(0, 5, 1, 6)
+    summary_tile(3)
+    w_cross(2, 7)
     join_block(1)
     w_cross(3, 8, 4, 9)
     attended_ready()

time: 74.3 us -> 74.3 us (level)
  no operation moved by 1% of the time
where the time goes in v5:
time: 74.3 us; the launch traced here: 74.1 us
  Pallas kernels  72.3 us (97%)
  other arithmetic  1.77 us (2%)
    pallas_call x1, Pallas kernels, body(): pl.pallas_call(kernel, out_shape=jax.ShapeDtypeStruct((64, 2048), F32), i...  72.3 us
    convert_element_type x1, other arithmetic, body(): return pl.pallas_call(kernel, out_shape=jax.ShapeDtypeStruct((64, 2048),...  1.77 us

profile of v5, /device:TPU:27, one launch (start us, length us, event | category | flops | bytes accessed | tf_op | source)
XLA Modules:
  0.0 74.1 jit_solution(16378966596512183059)
XLA Ops:
  0.0 72.3 %shard_map.46 = f32[64,2048]{1,0:T(8,128)} custom-call(bf16[1024,128]{1,0:T(8,128)(2,1)} %q_hbm.1, bf16[1024,128]{1,0:T(8,128)(2,1)} %k_hbm.1, bf16[1024,128]{1,0:T(8,128)(2,1)} %v_hbm.1, bf16[128,2048]{1,0:T(8,128)(2,1)} %w_hbm.1), custom_call_target="tpu_custom_call" | custom-call | tf_op jit(solution)/shard_map/pallas_call | solution.py:457
  72.4 1.8 %convert_element_type.3 = bf16[64,2048]{1,0:T(8,128)(2,1)} convert(f32[64,2048]{1,0:T(8,128)} %shard_map.46) | non-fusion elementwise | flops 131072 | bytes 786432 | tf_op jit(solution)/shard_map/convert_element_type | solution.py:486
